TPU v7x, 32 devices: a whole 2x2x4 slice. The times are simulated.
32 devices in a mesh: groups: 2 (over x), tensor: 16 (over z, y, core).
Axes of the slice: x: 2, y: 2, z: 4, core: 2. Of those that a mesh axis runs over, the one named last changes fastest.
Arguments:
- queries: bfloat16 [16, 16384], P('groups', 'tensor'), parts along dimension 0, may hold values from -120 to 120
- kv_cache: bfloat16 [2, 16, 512, 1024], P(None, 'groups', 'tensor'), parts along dimension 1, may hold values from -4 to 4
- lengths: int32 [16], P('groups'), parts along dimension 0, may hold values from 2 to 512, as said below
- out_weight: bfloat16 [16384, 16384], P('tensor'), may hold values from -0.8984375 to 0.8984375
- outlier_values: bfloat16 [128, 4, 128, 128], P('tensor'), may hold values from -3 to 3
- outlier_columns: int32 [128, 4], P('tensor'), may hold values from 0 to 127
- outlier_counts: int32 [128], P('tensor'), may hold values from 1 to 4, as said below
Outputs:
- mixed: bfloat16 [16, 16384], P('groups', 'tensor'), parts along dimension 0
There are 2 independent parts, one for each index of `groups`. A program takes and returns all parts, laid end to end along the dimension named above; an argument that names none is the same for every part. Nothing has to cross between parts.
Inputs may be any that keep to these rules, and one draw needn't show every extreme that they name: `lengths`: some request has all 512 positions live and some has 2. `outlier_counts`: some head has all 4 slots live and some has one.
All inputs are finite; a program needn't handle non-finite values.
Results may differ from a plain program's by a relative error of at most 0.0057.
Values may be sent and summed in bfloat16 or wider, within the bound.
A program may use at most 128 MiB of HBM per device.

v0:
```python
import math

import jax
import jax.numpy as jnp
from jax import lax
from jax.sharding import PartitionSpec as P

D = 16384
KVH = 8
HD = 128
OBLK = 128
OMAX = 4


def body(queries, kv_cache, lengths, out_weight, outlier_values, outlier_columns, outlier_counts):
    row_count = queries.shape[0]
    device_count = lax.axis_size("tensor")
    local_heads = queries.shape[1] // HD
    positions = kv_cache.shape[2]
    seq_total = positions * device_count
    keyvals = kv_cache.reshape(2, row_count, positions, KVH, HD)
    copies = device_count // KVH
    picked = jnp.broadcast_to(
        keyvals[:, :, :, :, None, :], (2, row_count, positions, KVH, copies, HD)
    )
    picked = picked.reshape(2, row_count, positions, device_count, HD)
    received = lax.all_to_all(picked, "tensor", split_axis=3, concat_axis=2, tiled=True)
    received = received.reshape(2, row_count, seq_total, HD)
    queried = queries.reshape(row_count, local_heads, HD)
    scores = jnp.einsum(
        "rhd,rsd->rhs", queried, received[0], preferred_element_type=jnp.float32
    ) / math.sqrt(HD)
    visible = jnp.arange(seq_total, dtype=jnp.int32)[None, :] < lengths[:, None]
    scores = jnp.where(visible[:, None, :], scores, -1e30)
    row_peak = jnp.max(scores, axis=-1, keepdims=True)
    raised = jnp.exp(scores - row_peak)
    totals = jnp.sum(raised, axis=-1, keepdims=True)
    weights = (raised / totals).astype(jnp.bfloat16)
    attended = jnp.einsum("rhs,rsd->rhd", weights, received[1], preferred_element_type=jnp.float32)
    attended = attended.astype(jnp.bfloat16).reshape(row_count, local_heads * HD)
    blocks = D // OBLK
    slot_live = jnp.arange(OMAX, dtype=jnp.int32)[None, :] < outlier_counts[:, None]
    placement = (
        (outlier_columns[:, :, None] == jnp.arange(blocks, dtype=jnp.int32)[None, None, :])
        & slot_live[:, :, None]
    ).astype(jnp.bfloat16)
    projected = jnp.dot(attended, out_weight, preferred_element_type=jnp.float32)
    heads_attended = attended.reshape(row_count, local_heads, HD)
    outlier_terms = jnp.einsum(
        "rhd,hodc->rhoc", heads_attended, outlier_values, preferred_element_type=jnp.float32
    )
    correction = jnp.einsum("rhoc,hob->rbc", outlier_terms, placement.astype(jnp.float32)).reshape(
        row_count, D
    )
    summed = projected + correction
    mixed = lax.psum_scatter(summed, "tensor", scatter_dimension=1, tiled=True)
    return mixed.astype(jnp.bfloat16)


def solution(mesh):
    placed = (
        P("groups", "tensor"),
        P(None, "groups", "tensor", None),
        P("groups"),
        P("tensor", None),
        P("tensor", None, None, None),
        P("tensor", None),
        P("tensor"),
    )
    return jax.shard_map(
        body, mesh=mesh, in_specs=placed, out_specs=P("groups", "tensor"), check_vma=False
    )
```

profile of v0, /device:TPU:0, one launch (start us, length us, event | category | flops | bytes accessed | tf_op | source)
XLA Modules:
  0.0 148.2 jit_solution(8957795780256192172)
XLA Ops:
  6.5 0.0 copy-start
  6.5 1.2 copy-done
  7.8 0.3 copy_bitcast_fusion
  8.0 1.8 %broadcast_in_dim.18 = bf16[2,8,32,8,2,128]{5,2,1,0,4,3:T(8,128)(2,1)} broadcast(bf16[2,8,32,8,128]{4,2,1,0,3:T(8,128)(2,1)S(1)} %copy_bitcast_fusion), dimensions={0,1,2,3,5} | broadcast | bytes 3145728 | tf_op jit(solution)/shard_map/broadcast_in_dim | solution.py:23
  9.9 7.4 %all-to-all-start = ((bf16[2,8,32,16,128]{4,2,1,0,3:T(8,128)(2,1)}), bf16[2,8,32,16,128]{4,2,1,0,3:T(8,128)(2,1)S(1)}, u32[]{:S(2)}, u32[]{:S(2)}) async-start(bf16[2,8,32,16,128]{4,2,1,0,3:T(8,128)(2,1)} %bitcast.38), calls=%async_computation | async-start | bytes 4194304 | tf_op jit(solution)/shard_map/all_to_all | solution.py:27
  17.3 0.0 reduce-scatter.2.cloned.1.call-start
  17.3 0.7 iota_compare_fusion.2
  18.0 0.7 iota_compare_fusion.1
  18.7 39.5 %all-to-all-done = bf16[2,8,32,16,128]{4,2,1,0,3:T(8,128)(2,1)S(1)} async-done(((bf16[2,8,32,16,128]{4,2,1,0,3:T(8,128)(2,1)}), bf16[2,8,32,16,128]{4,2,1,0,3:T(8,128)(2,1)S(1)}, u32[]{:S(2)}, u32[]{:S(2)}) %all-to-all-start) | async-done | bytes 2097184 | tf_op jit(solution)/shard_map/all_to_all | solution.py:27
  58.3 0.5 fusion.17
  58.8 0.1 copy.11
  58.9 1.1 fusion.3
  60.0 0.2 fusion.18
  60.2 0.1 copy.13
  60.3 0.3 convolution_convert_fusion
  60.6 1.5 fusion.9
  62.0 1.0 convolution_bitcast_fusion
  63.1 13.9 %convolution_add_fusion = f32[8,16384]{1,0:T(8,128)} fusion(bf16[1024,16384]{1,0:T(8,128)(2,1)} %param.10, f32[1,8,128,128]{3,2,1,0:T(8,128)S(1)} %convolution_bitcast_fusion, bf16[1,8,8,128]{3,2,1,0:T(8,128)(2,1)S(1)} %bitcast.42), kind=kOutput, calls=%fused_computation.1 | convolution fusion | flops 268566528 | bytes 34619392 | tf_op jit(solution)/shard_map/dot_general | solution.py:47
  77.0 0.0 reduce-scatter.2.cloned.1.call-update
  77.0 62.9 %reduce-scatter.2.cloned.1.call-done = f32[8,1024]{1,0:T(8,128)} async-done(((f32[8,16384]{1,0:T(8,128)}), f32[8,1024]{1,0:T(8,128)}) %reduce-scatter.2.cloned.1.call-update) | async-done | bytes 32784 | tf_op jit(solution)/shard_map/reduce_scatter | solution.py:56
  139.9 1.4 convert_element_type.13
Async XLA Ops:
  6.5 1.2 copy-start
  9.9 48.4 %all-to-all-start = ((bf16[2,8,32,16,128]{4,2,1,0,3:T(8,128)(2,1)}), bf16[2,8,32,16,128]{4,2,1,0,3:T(8,128)(2,1)S(1)}, u32[]{:S(2)}, u32[]{:S(2)}) async-start(bf16[2,8,32,16,128]{4,2,1,0,3:T(8,128)(2,1)} %bitcast.38), calls=%async_computation | async-start | bytes 4194304 | tf_op jit(solution)/shard_map/all_to_all | solution.py:27
  17.3 122.7 %reduce-scatter.2.cloned.1.call-start = ((), (), s32[]{:S(2)}) async-start(), calls=%async_computation.2 | async-start | bytes 557056 | tf_op jit(solution)/shard_map/reduce_scatter | solution.py:56
Sparse Core Ops, SparseCore 0:
  77.1 62.7 reduce-scatter.1
where the time goes:
time: 149 us; the launch traced here: 148 us
  waiting for transfers between devices  102 us (68%)
  matrix products  17.8 us (12%)
  between operations  13.5 us (9%)
  starting transfers between devices  7.46 us (5%)
  local copies, waits for them, and re-layouts  4 us (3%)
  other arithmetic  2.95 us (2%)
    reduce_scatter x1, waiting for transfers between devices, body(): mixed = lax.psum_scatter(summed, 'tensor', scatter_dimension=1, tiled=True)  62.9 us
    all_to_all x1, waiting for transfers between devices, body(): lax.all_to_all(picked, 'tensor', split_axis=3, concat_axis=2, tiled=True)  39.5 us
    dot_general x1, matrix products, body(): jnp.dot(attended, out_weight, preferred_element_type=jnp.float32)  13.9 us
    all_to_all x1, starting transfers between devices, body(): lax.all_to_all(picked, 'tensor', split_axis=3, concat_axis=2, tiled=True)  7.41 us
  transfers between devices with their start and end apart: 2, of which 2 were waited for; matrix products, arithmetic and copies ran while one was open for 1% of the time, Pallas kernels for 0%

commit v1 on v0

v1 whole, which is shorter than its diff:
```python
import functools
import math

import jax
import jax.numpy as jnp
from jax import lax
from jax.experimental import pallas as pl
from jax.experimental.pallas import tpu as pltpu
from jax.sharding import PartitionSpec as P

KVH = 8
HD = 128
STAT = 16
MESH = pl.DeviceIdType.MESH
F32 = jnp.float32
BF16 = jnp.bfloat16


def flip(a, b, n):
    out, bit = 0, 1
    while bit < n:
        out = out + ((a // bit + b // bit) % 2) * bit
        bit *= 2
    return out


def kernel(
    n,
    q_hbm, kv_hbm, w_hbm, ov_hbm, len_ref, col_ref, cnt_ref,
    out_ref,
    qbuf, kvbuf, wbuf, ovbuf, bias, osend, obuf, abuf, tbuf, sbuf, rbuf,
    kv_sem, kvs_sem, kvr_sem, qs_sem, qr_sem, w_sem, ov_sem, os_sem, or_sem, ss_sem, sr_sem,
):
    me = lax.axis_index("tensor")
    core = me % 2
    chip = me // 2
    partner = me + 1 - 2 * core
    chips = n // 2
    half = me // chips
    rows, width = q_hbm.shape
    hl = width // HD
    nr = hl * rows
    g = n // KVH
    kh = KVH // 2
    positions = kv_hbm.shape[2]
    cols = w_hbm.shape[1] // n
    omax = ov_hbm.shape[1]
    jb = cols // HD
    hw = kh * HD
    kvcols = rows * positions

    def kv_half(c):
        return kv_hbm.at[:, :, :, pl.ds(pl.multiple_of(c * hw, hw), hw)]

    kv_own = pltpu.make_async_copy(kv_half(core), kvbuf.at[0], kv_sem)
    kv_own.start()
    ov_copy = pltpu.make_async_copy(ov_hbm, ovbuf, ov_sem)
    my_slot = me - half * chips

    barrier = pltpu.get_barrier_semaphore()

    @pl.loop(1, n)
    def _(i):
        pl.semaphore_signal(barrier, inc=1, device_id={"tensor": flip(me, i, n)}, device_id_type=MESH)

    @pl.when(half == core)
    def _():
        pltpu.make_async_copy(q_hbm, qbuf.at[my_slot], qr_sem.at[my_slot]).start()

    def w_copy(i):
        dest = flip(me, n - 1 - i, n)
        return pltpu.make_async_copy(
            w_hbm.at[:, pl.ds(pl.multiple_of(dest * cols, cols), cols)], wbuf.at[i], w_sem.at[i]
        )

    rowreq = lax.broadcasted_iota(jnp.int32, (g * nr, kvcols), 0) % rows
    colidx = lax.broadcasted_iota(jnp.int32, (1, kvcols), 1)
    colreq = colidx // positions
    limit = jnp.zeros((1, kvcols), jnp.int32)
    for r in range(rows):
        limit = jnp.where(colreq == r, len_ref[r], limit)
    for part in range(2):
        dev = me if part == 0 else partner
        live = (colidx % positions + dev * positions) < limit
        tag = jnp.where(live, colreq, -1)
        bias[part] = jnp.where(rowreq == tag, 0.0, -1e30).astype(F32)

    pl.semaphore_wait(barrier, n - 1)

    swap = pltpu.make_async_remote_copy(
        src_ref=kv_half(1 - core), dst_ref=kvbuf.at[1], send_sem=kvs_sem, recv_sem=kvr_sem,
        device_id={"tensor": partner}, device_id_type=MESH,
    )
    swap.start()

    def q_send(i):
        p = flip(chip, chips - 1 - i, chips)
        target = 2 * p + half
        return target, pltpu.make_async_remote_copy(
            src_ref=q_hbm, dst_ref=qbuf.at[my_slot], send_sem=qs_sem.at[i], recv_sem=qr_sem.at[my_slot],
            device_id={"tensor": target}, device_id_type=MESH,
        )

    @pl.loop(0, chips)
    def _(i):
        target, copy = q_send(i)

        @pl.when(target != me)
        def _():
            copy.start()

    @pl.loop(0, n)
    def _(i):
        w_copy(i).start()

    ov_copy.start()

    kv_own.wait()
    swap.wait()

    eye = lax.broadcasted_iota(jnp.int32, (g * nr, HD), 0) == lax.broadcasted_iota(jnp.int32, (g * nr, HD), 1)
    stat_row = lax.broadcasted_iota(jnp.int32, (STAT, HD), 0)

    def to_row(column):
        return jnp.sum(jnp.where(eye, column, 0.0), axis=0, keepdims=True)

    def o_send(j):
        target = core * chips + j
        return target, pltpu.make_async_remote_copy(
            src_ref=osend.at[j], dst_ref=obuf.at[chip], send_sem=os_sem.at[j], recv_sem=or_sem.at[chip],
            device_id={"tensor": target}, device_id_type=MESH,
        )

    def o_local(j):
        return pltpu.make_async_copy(osend.at[j], obuf.at[chip], or_sem.at[chip])

    for kl in range(kh):
        pieces = []
        for dl in range(g):
            slot = kl * g + dl
            pltpu.make_async_copy(qbuf.at[slot], qbuf.at[slot], qr_sem.at[slot]).wait()
            got = qbuf[slot].astype(F32)
            pieces += [got[:, h * HD:(h + 1) * HD] for h in range(hl)]
        q = jnp.concatenate(pieces, axis=0).astype(BF16)
        scores, values = [], []
        for part in range(2):
            keys = kvbuf[part, 0, :, :, kl * HD:(kl + 1) * HD].reshape(kvcols, HD)
            values.append(kvbuf[part, 1, :, :, kl * HD:(kl + 1) * HD].reshape(kvcols, HD))
            s = lax.dot_general(q, keys, (((1,), (1,)), ((), ())), preferred_element_type=F32)
            scores.append(s * (1.0 / math.sqrt(HD)) + bias[part])
        peak = jnp.maximum(
            jnp.max(scores[0], axis=-1, keepdims=True), jnp.max(scores[1], axis=-1, keepdims=True)
        )
        peak = jnp.maximum(peak, -(2.0**66)).astype(BF16).astype(F32)
        total = jnp.zeros((g * nr, 1), F32)
        o = jnp.zeros((g * nr, HD), F32)
        for part in range(2):
            raised = jnp.exp(scores[part] - peak)
            total = total + jnp.sum(raised, axis=-1, keepdims=True)
            o = o + jnp.dot(raised.astype(BF16), values[part], preferred_element_type=F32)
        total_row = to_row(total)
        total_hi = total_row.astype(BF16).astype(F32)
        stats = jnp.where(
            stat_row == 0, to_row(peak), jnp.where(stat_row == 1, total_hi, total_row - total_hi)
        ).astype(BF16)
        o = o.astype(BF16)
        for dl in range(g):
            slot = kl * g + dl
            osend[slot, :nr, :] = o[dl * nr:(dl + 1) * nr]
            osend[slot, nr:, :] = stats
            target, copy = o_send(slot)

            @pl.when(target != me)
            def _():
                copy.start()

            @pl.when(target == me)
            def _():
                o_local(slot).start()

    for p in range(chips):
        pltpu.make_async_copy(obuf.at[p], obuf.at[p], or_sem.at[p]).wait()
    peaks, totals = [], []
    for p in range(chips):
        st = obuf[p, nr:, :].astype(F32)
        peaks.append(st[0:1])
        totals.append(st[1:2] + st[2:3])
    peak = functools.reduce(jnp.maximum, peaks)
    shares = [jnp.exp(m - peak) for m in peaks]
    total = sum(s * t for s, t in zip(shares, totals))
    first = (me % g) * nr
    mine = (
        lax.broadcasted_iota(jnp.int32, (nr, HD), 0) + first
        == lax.broadcasted_iota(jnp.int32, (nr, HD), 1)
    )
    attended = jnp.zeros((nr, HD), F32)
    for p in range(chips):
        share = jnp.sum(jnp.where(mine, shares[p] / total, 0.0), axis=1, keepdims=True)
        attended = attended + share * obuf[p, :nr, :].astype(F32)
    a = jnp.concatenate([attended[h * rows:(h + 1) * rows] for h in range(hl)], axis=1).astype(BF16)
    abuf[...] = a

    ov_copy.wait()
    for h in range(hl):
        for o in range(omax):
            tbuf[h * omax + o] = jnp.dot(
                a[:, h * HD:(h + 1) * HD], ovbuf[h, o], preferred_element_type=F32
            )

    def block(i):
        dest = flip(me, n - 1 - i, n)
        w_copy(i).wait()
        part = jnp.dot(abuf[...], wbuf[i], preferred_element_type=F32)
        sums = [part[:, j * HD:(j + 1) * HD] for j in range(jb)]
        for h in range(hl):
            for o in range(omax):
                col = jnp.where(o < cnt_ref[h], col_ref[h, o] - dest * jb, -1)
                colv = jnp.full((rows, HD), col, jnp.int32)
                term = tbuf[h * omax + o]
                sums = [s + jnp.where(colv == j, term, 0.0) for j, s in enumerate(sums)]
        return dest, jnp.concatenate(sums, axis=1)

    def s_send(i, dest):
        return pltpu.make_async_remote_copy(
            src_ref=sbuf.at[i], dst_ref=rbuf.at[i], send_sem=ss_sem.at[i], recv_sem=sr_sem.at[i],
            device_id={"tensor": dest}, device_id_type=MESH,
        )

    @pl.loop(0, n - 1)
    def _(i):
        dest, sums = block(i)
        sbuf[i] = sums.astype(sbuf.dtype)
        s_send(i, dest).start()

    _, acc = block(n - 1)


    @pl.loop(0, chips)
    def _(i):
        target, copy = q_send(i)

        @pl.when(target != me)
        def _():
            copy.wait_send()

        target2, copy2 = o_send(i)

        @pl.when(target2 != me)
        def _():
            copy2.wait_send()

    def gather(i, acc):
        dest = flip(me, n - 1 - i, n)
        s_send(i, dest).wait()
        return acc + rbuf[i].astype(F32)

    out_ref[...] = lax.fori_loop(0, n - 1, gather, acc)


def body(n, queries, kv_cache, lengths, out_weight, outlier_values, outlier_columns, outlier_counts):
    rows, width = queries.shape
    hl = width // HD
    nr = hl * rows
    positions = kv_cache.shape[2]
    cols = out_weight.shape[1] // n
    omax = outlier_values.shape[1]
    chips = n // 2
    g = n // KVH
    dma = pltpu.SemaphoreType.DMA
    out = pl.pallas_call(
        functools.partial(kernel, n),
        out_shape=jax.ShapeDtypeStruct((rows, cols), F32),
        in_specs=[pl.BlockSpec(memory_space=pl.ANY)] * 4 + [pl.BlockSpec(memory_space=pltpu.SMEM)] * 3,
        out_specs=pl.BlockSpec(memory_space=pltpu.VMEM),
        scratch_shapes=[
            pltpu.VMEM((chips, rows, width), BF16),
            pltpu.VMEM((2, 2, rows, positions, KVH // 2 * HD), BF16),
            pltpu.VMEM((n, width, cols), BF16),
            pltpu.VMEM(outlier_values.shape, BF16),
            pltpu.VMEM((2, g * nr, rows * positions), F32),
            pltpu.VMEM((chips, nr + STAT, HD), BF16),
            pltpu.VMEM((chips, nr + STAT, HD), BF16),
            pltpu.VMEM((rows, width), BF16),
            pltpu.VMEM((hl * omax, rows, HD), F32),
            pltpu.VMEM((n, rows, cols), BF16),
            pltpu.VMEM((n, rows, cols), BF16),
            dma, dma, dma, dma((chips,)), dma((chips,)), dma((n,)), dma, dma((chips,)), dma((chips,)),
            dma((n,)), dma((n,)),
        ],
        compiler_params=pltpu.CompilerParams(
            collective_id=0, has_side_effects=True, vmem_limit_bytes=60 * 2**20
        ),
    )(queries, kv_cache, out_weight, outlier_values, lengths, outlier_columns, outlier_counts)
    return out.astype(BF16)


def solution(mesh):
    placed = (
        P("groups", "tensor"),
        P(None, "groups", "tensor", None),
        P("groups"),
        P("tensor", None),
        P("tensor", None, None, None),
        P("tensor", None),
        P("tensor"),
    )
    return jax.shard_map(
        functools.partial(body, mesh.shape["tensor"]),
        mesh=mesh, in_specs=placed, out_specs=P("groups", "tensor"), check_vma=False,
    )
```

time: 149 us -> 32.1 us (0.22)
  waiting for transfers between devices: 102 us -> 0 us
  Pallas kernels: 0 us -> 29.1 us
  matrix products: 17.8 us -> 0 us
  between operations: 13.5 us -> 0.01 us
  starting transfers between devices: 7.46 us -> 0 us
  local copies, waits for them, and re-layouts: 4 us -> 1.35 us
  other arithmetic: 2.95 us -> 1.37 us
    reduce_scatter x1 -> x0, waiting for transfers between devices: 62.9 us -> none  [body(): mixed = lax.psum_scatter(summed, 'tensor', scatter_dimension=1, tiled=True)]
    all_to_all x1 -> x0, waiting for transfers between devices: 39.5 us -> none  [body(): lax.all_to_all(picked, 'tensor', split_axis=3, concat_axis=2, tiled=True)]
    pallas_call x0 -> x1, Pallas kernels: none -> 29.1 us  [body(): pl.pallas_call(functools.partial(kernel, n), out_shape=jax.ShapeDtypeStru...]
    dot_general x5 -> x0, matrix products: 17.8 us -> none  [the longest x1 13.9 us: body(): jnp.dot(attended, out_weight, preferred_element_type=jnp.float32)]
    all_to_all x1 -> x0, starting transfers between devices: 7.41 us -> none  [body(): lax.all_to_all(picked, 'tensor', split_axis=3, concat_axis=2, tiled=True)]
    broadcast_in_dim x2 -> x0, local copies, waits for them, and re-layouts: 2.09 us -> none  [body(): jnp.broadcast_to(keyvals[:, :, :, :, None, :], (2, row_count, positions,...]
  transfers between devices with their start and end apart: 2 -> 0, of which waited for: 2 -> 0; matrix products, arithmetic and copies ran while one was open for 1% -> 0% of each run, Pallas kernels for 0% -> 0%
where the time goes in v1:
time: 32.1 us; the launch traced here: 31.8 us
  Pallas kernels  29.1 us (91%)
  other arithmetic  1.37 us (4%)
  local copies, waits for them, and re-layouts  1.35 us (4%)
    pallas_call x1, Pallas kernels, body(): pl.pallas_call(functools.partial(kernel, n), out_shape=jax.ShapeDtypeStru...  29.1 us
    convert_element_type x1, other arithmetic, body(): return out.astype(BF16)  1.37 us
    unnamed x1, local copies, waits for them, and re-layouts  1.35 us

profile of v1, /device:TPU:0, one launch (start us, length us, event | category | flops | bytes accessed | tf_op | source)
XLA Modules:
  0.0 31.8 jit_solution(15689756065493797334)
XLA Ops:
  0.0 1.3 %copy.8.col_ref = s32[8,4]{1,0:T(8,128)} copy(s32[8,4]{0,1:T(4,128)} %param.12) | data formatting | bytes 256 | tf_op args[5]
  1.3 29.1 %shard_map.73 = f32[8,1024]{1,0:T(8,128)} custom-call(bf16[8,1024]{1,0:T(8,128)(2,1)} %q_hbm.1, bf16[2,8,32,1024]{3,2,1,0:T(8,128)(2,1)} %kv_hbm.1, bf16[1024,16384]{1,0:T(8,128)(2,1)} %w_hbm.1, bf16[8,4,128,128]{3,2,1,0:T(8,128)(2,1)} %ov_hbm.1, s32[8]{0:T(128)} %len_ref.1, s32[8,4]{1,0:T(8,128)} %copy.8.col_ref, s32[8]{0:T(128)} %cnt_ref.1), custom_call_target="tpu_custom_call" | custom-call | tf_op jit(solution)/shard_map/pallas_call | solution.py:270
  30.5 1.4 %convert_element_type.3 = bf16[8,1024]{1,0:T(8,128)(2,1)} convert(f32[8,1024]{1,0:T(8,128)} %shard_map.73) | non-fusion elementwise | flops 8192 | bytes 49152 | tf_op jit(solution)/shard_map/convert_element_type | solution.py:294

commit v2 on v1

--- a/solution.py
+++ b/solution.py
@@ -26,10 +26,10 @@
 
 def kernel(
     n,
-    q_hbm, kv_hbm, w_hbm, ov_hbm, len_ref, col_ref, cnt_ref,
+    q_hbm, kv_hbm, w_hbm, ov_hbm, len_hbm, col_hbm, cnt_hbm,
     out_ref,
-    qbuf, kvbuf, wbuf, ovbuf, bias, osend, obuf, abuf, tbuf, sbuf, rbuf,
-    kv_sem, kvs_sem, kvr_sem, qs_sem, qr_sem, w_sem, ov_sem, os_sem, or_sem, ss_sem, sr_sem,
+    len_ref, col_ref, cnt_ref, qbuf, kvbuf, wbuf, ovbuf, bias, osend, obuf, abuf, tbuf, psend, precv, sbuf, rbuf,
+    small_sem, kv_sem, kvs_sem, kvr_sem, qs_sem, qr_sem, w_sem, ov_sem, os_sem, or_sem, ps_sem, pr_sem, ss_sem, sr_sem,
 ):
     me = lax.axis_index("tensor")
     core = me % 2
@@ -49,29 +49,36 @@
     hw = kh * HD
     kvcols = rows * positions
 
+    barrier = pltpu.get_barrier_semaphore()
+    for i in range(n - 1, 0, -1):
+        pl.semaphore_signal(barrier, inc=1, device_id={"tensor": flip(me, i, n)}, device_id_type=MESH)
+
     def kv_half(c):
         return kv_hbm.at[:, :, :, pl.ds(pl.multiple_of(c * hw, hw), hw)]
 
+    small = [
+        pltpu.make_async_copy(src, dst, small_sem.at[i])
+        for i, (src, dst) in enumerate(((len_hbm, len_ref), (col_hbm, col_ref), (cnt_hbm, cnt_ref)))
+    ]
+    for copy in small:
+        copy.start()
     kv_own = pltpu.make_async_copy(kv_half(core), kvbuf.at[0], kv_sem)
     kv_own.start()
     ov_copy = pltpu.make_async_copy(ov_hbm, ovbuf, ov_sem)
     my_slot = me - half * chips
 
-    barrier = pltpu.get_barrier_semaphore()
-
-    @pl.loop(1, n)
-    def _(i):
-        pl.semaphore_signal(barrier, inc=1, device_id={"tensor": flip(me, i, n)}, device_id_type=MESH)
-
     @pl.when(half == core)
     def _():
         pltpu.make_async_copy(q_hbm, qbuf.at[my_slot], qr_sem.at[my_slot]).start()
 
     def w_copy(i):
-        dest = flip(me, n - 1 - i, n)
+        dest = 2 * flip(chip, chips - 1 - i // 2, chips) + (core + 1 + i % 2) % 2
         return pltpu.make_async_copy(
             w_hbm.at[:, pl.ds(pl.multiple_of(dest * cols, cols), cols)], wbuf.at[i], w_sem.at[i]
         )
+
+    for copy in small:
+        copy.wait()
 
     rowreq = lax.broadcasted_iota(jnp.int32, (g * nr, kvcols), 0) % rows
     colidx = lax.broadcasted_iota(jnp.int32, (1, kvcols), 1)
@@ -85,6 +92,12 @@
         tag = jnp.where(live, colreq, -1)
         bias[part] = jnp.where(rowreq == tag, 0.0, -1e30).astype(F32)
 
+    ov_copy.start()
+
+    @pl.loop(0, n)
+    def _(i):
+        w_copy(i).start()
+
     pl.semaphore_wait(barrier, n - 1)
 
     swap = pltpu.make_async_remote_copy(
@@ -109,12 +122,6 @@
         def _():
             copy.start()
 
-    @pl.loop(0, n)
-    def _(i):
-        w_copy(i).start()
-
-    ov_copy.start()
-
     kv_own.wait()
     swap.wait()
 
@@ -134,7 +141,10 @@
     def o_local(j):
         return pltpu.make_async_copy(osend.at[j], obuf.at[chip], or_sem.at[chip])
 
-    for kl in range(kh):
+    upper = chip // (chips // 2)
+    for step in range(kh):
+        kl = step + upper * (kh - 1 - 2 * step)
+        lanes = pl.ds(pl.multiple_of(kl * HD, HD), HD)
         pieces = []
         for dl in range(g):
             slot = kl * g + dl
@@ -144,8 +154,8 @@
         q = jnp.concatenate(pieces, axis=0).astype(BF16)
         scores, values = [], []
         for part in range(2):
-            keys = kvbuf[part, 0, :, :, kl * HD:(kl + 1) * HD].reshape(kvcols, HD)
-            values.append(kvbuf[part, 1, :, :, kl * HD:(kl + 1) * HD].reshape(kvcols, HD))
+            keys = kvbuf[part, 0, :, :, lanes].reshape(kvcols, HD)
+            values.append(kvbuf[part, 1, :, :, lanes].reshape(kvcols, HD))
             s = lax.dot_general(q, keys, (((1,), (1,)), ((), ())), preferred_element_type=F32)
             scores.append(s * (1.0 / math.sqrt(HD)) + bias[part])
         peak = jnp.maximum(
@@ -208,32 +218,45 @@
             )
 
     def block(i):
-        dest = flip(me, n - 1 - i, n)
+        dest = 2 * flip(chip, chips - 1 - i // 2, chips) + (core + 1 + i % 2) % 2
         w_copy(i).wait()
         part = jnp.dot(abuf[...], wbuf[i], preferred_element_type=F32)
         sums = [part[:, j * HD:(j + 1) * HD] for j in range(jb)]
         for h in range(hl):
             for o in range(omax):
-                col = jnp.where(o < cnt_ref[h], col_ref[h, o] - dest * jb, -1)
+                col = jnp.where(o < cnt_ref[h], col_ref[o, h] - dest * jb, -1)
                 colv = jnp.full((rows, HD), col, jnp.int32)
                 term = tbuf[h * omax + o]
                 sums = [s + jnp.where(colv == j, term, 0.0) for j, s in enumerate(sums)]
-        return dest, jnp.concatenate(sums, axis=1)
-
-    def s_send(i, dest):
+        return jnp.concatenate(sums, axis=1)
+
+    def p_send(i):
+        return pltpu.make_async_remote_copy(
+            src_ref=psend.at[i], dst_ref=precv.at[i], send_sem=ps_sem.at[i], recv_sem=pr_sem.at[i],
+            device_id={"tensor": partner}, device_id_type=MESH,
+        )
+
+    def s_send(i):
         return pltpu.make_async_remote_copy(
             src_ref=sbuf.at[i], dst_ref=rbuf.at[i], send_sem=ss_sem.at[i], recv_sem=sr_sem.at[i],
-            device_id={"tensor": dest}, device_id_type=MESH,
-        )
-
-    @pl.loop(0, n - 1)
+            device_id={"tensor": 2 * flip(chip, chips - 1 - i, chips) + core}, device_id_type=MESH,
+        )
+
+    psend[0] = block(0)
+    p_send(0).start()
+
+    @pl.loop(0, chips - 1)
     def _(i):
-        dest, sums = block(i)
-        sbuf[i] = sums.astype(sbuf.dtype)
-        s_send(i, dest).start()
-
-    _, acc = block(n - 1)
-
+        psend[i + 1] = block(2 * i + 2)
+        p_send(i + 1).start()
+        sums = block(2 * i + 1)
+        p_send(i).wait_recv()
+        sbuf[i] = (sums + precv[i]).astype(sbuf.dtype)
+        s_send(i).start()
+
+    acc = block(n - 1)
+    p_send(chips - 1).wait_recv()
+    acc = acc + precv[chips - 1]
 
     @pl.loop(0, chips)
     def _(i):
@@ -249,12 +272,13 @@
         def _():
             copy2.wait_send()
 
+        p_send(i).wait_send()
+
     def gather(i, acc):
-        dest = flip(me, n - 1 - i, n)
-        s_send(i, dest).wait()
+        s_send(i).wait()
         return acc + rbuf[i].astype(F32)
 
-    out_ref[...] = lax.fori_loop(0, n - 1, gather, acc)
+    out_ref[...] = lax.fori_loop(0, chips - 1, gather, acc)
 
 
 def body(n, queries, kv_cache, lengths, out_weight, outlier_values, outlier_columns, outlier_counts):
@@ -270,9 +294,12 @@
     out = pl.pallas_call(
         functools.partial(kernel, n),
         out_shape=jax.ShapeDtypeStruct((rows, cols), F32),
-        in_specs=[pl.BlockSpec(memory_space=pl.ANY)] * 4 + [pl.BlockSpec(memory_space=pltpu.SMEM)] * 3,
+        in_specs=[pl.BlockSpec(memory_space=pl.ANY)] * 7,
         out_specs=pl.BlockSpec(memory_space=pltpu.VMEM),
         scratch_shapes=[
+            pltpu.SMEM(lengths.shape, jnp.int32),
+            pltpu.SMEM((omax, hl), jnp.int32),
+            pltpu.SMEM(outlier_counts.shape, jnp.int32),
             pltpu.VMEM((chips, rows, width), BF16),
             pltpu.VMEM((2, 2, rows, positions, KVH // 2 * HD), BF16),
             pltpu.VMEM((n, width, cols), BF16),
@@ -282,15 +309,17 @@
             pltpu.VMEM((chips, nr + STAT, HD), BF16),
             pltpu.VMEM((rows, width), BF16),
             pltpu.VMEM((hl * omax, rows, HD), F32),
-            pltpu.VMEM((n, rows, cols), BF16),
-            pltpu.VMEM((n, rows, cols), BF16),
-            dma, dma, dma, dma((chips,)), dma((chips,)), dma((n,)), dma, dma((chips,)), dma((chips,)),
-            dma((n,)), dma((n,)),
+            pltpu.VMEM((chips, rows, cols), F32),
+            pltpu.VMEM((chips, rows, cols), F32),
+            pltpu.VMEM((chips, rows, cols), BF16),
+            pltpu.VMEM((chips, rows, cols), BF16),
+            dma((3,)), dma, dma, dma, dma((chips,)), dma((chips,)), dma((n,)), dma, dma((chips,)), dma((chips,)),
+            dma((chips,)), dma((chips,)), dma((chips,)), dma((chips,)),
         ],
         compiler_params=pltpu.CompilerParams(
             collective_id=0, has_side_effects=True, vmem_limit_bytes=60 * 2**20
         ),
-    )(queries, kv_cache, out_weight, outlier_values, lengths, outlier_columns, outlier_counts)
+    )(queries, kv_cache, out_weight, outlier_values, lengths, outlier_columns.T, outlier_counts)
     return out.astype(BF16)
 
 

time: 32.1 us -> 29.1 us (0.907)
  Pallas kernels: 29.1 us -> 27.5 us
  local copies, waits for them, and re-layouts: 1.35 us -> 0 us
    pallas_call x1, Pallas kernels: 29.1 us -> 27.5 us  [body(): pl.pallas_call(functools.partial(kernel, n), out_shape=jax.ShapeDtypeStru...]
    unnamed x1 -> x0, local copies, waits for them, and re-layouts: 1.35 us -> none
where the time goes in v2:
time: 29.1 us; the launch traced here: 28.9 us
  Pallas kernels  27.5 us (95%)
  other arithmetic  1.37 us (5%)
    pallas_call x1, Pallas kernels, body(): pl.pallas_call(functools.partial(kernel, n), out_shape=jax.ShapeDtypeStru...  27.5 us
    convert_element_type x1, other arithmetic, body(): return out.astype(BF16)  1.37 us

profile of v2, /device:TPU:0, one launch (start us, length us, event | category | flops | bytes accessed | tf_op | source)
XLA Modules:
  0.0 28.9 jit_solution(13721781107015618093)
XLA Ops:
  0.0 27.5 %shard_map.73 = f32[8,1024]{1,0:T(8,128)} custom-call(bf16[8,1024]{1,0:T(8,128)(2,1)} %q_hbm.1, bf16[2,8,32,1024]{3,2,1,0:T(8,128)(2,1)} %kv_hbm.1, bf16[1024,16384]{1,0:T(8,128)(2,1)} %w_hbm.1, bf16[8,4,128,128]{3,2,1,0:T(8,128)(2,1)} %ov_hbm.1, s32[8]{0:T(128)} %len_hbm.1, s32[4,8]{1,0:T(4,128)} %bitcast.1, s32[8]{0:T(128)} %cnt_hbm.1), custom_call_target="tpu_custom_call" | custom-call | tf_op jit(solution)/shard_map/pallas_call | solution.py:294
  27.5 1.4 %convert_element_type.3 = bf16[8,1024]{1,0:T(8,128)(2,1)} convert(f32[8,1024]{1,0:T(8,128)} %shard_map.73) | non-fusion elementwise | flops 8192 | bytes 49152 | tf_op jit(solution)/shard_map/convert_element_type | solution.py:323

commit v3 on v2

--- a/solution.py
+++ b/solution.py
@@ -245,7 +245,7 @@
     psend[0] = block(0)
     p_send(0).start()
 
-    @pl.loop(0, chips - 1)
+    @pl.loop(0, chips - 1, unroll=True)
     def _(i):
         psend[i + 1] = block(2 * i + 2)
         p_send(i + 1).start()

time: 29.1 us -> 28.8 us (0.990)
  no operation moved by 1% of the time
where the time goes in v3:
time: 28.8 us; the launch traced here: 28.6 us
  Pallas kernels  27.3 us (95%)
  other arithmetic  1.37 us (5%)
    pallas_call x1, Pallas kernels, body(): pl.pallas_call(functools.partial(kernel, n), out_shape=jax.ShapeDtypeStru...  27.3 us
    convert_element_type x1, other arithmetic, body(): return out.astype(BF16)  1.37 us

profile of v3, /device:TPU:0, one launch (start us, length us, event | category | flops | bytes accessed | tf_op | source)
XLA Modules:
  0.0 28.6 jit_solution(7048631520362127355)
XLA Ops:
  0.0 27.3 %shard_map.73 = f32[8,1024]{1,0:T(8,128)} custom-call(bf16[8,1024]{1,0:T(8,128)(2,1)} %q_hbm.1, bf16[2,8,32,1024]{3,2,1,0:T(8,128)(2,1)} %kv_hbm.1, bf16[1024,16384]{1,0:T(8,128)(2,1)} %w_hbm.1, bf16[8,4,128,128]{3,2,1,0:T(8,128)(2,1)} %ov_hbm.1, s32[8]{0:T(128)} %len_hbm.1, s32[4,8]{1,0:T(4,128)} %bitcast.1, s32[8]{0:T(128)} %cnt_hbm.1), custom_call_target="tpu_custom_call" | custom-call | tf_op jit(solution)/shard_map/pallas_call | solution.py:294
  27.3 1.4 %convert_element_type.3 = bf16[8,1024]{1,0:T(8,128)(2,1)} convert(f32[8,1024]{1,0:T(8,128)} %shard_map.73) | non-fusion elementwise | flops 8192 | bytes 49152 | tf_op jit(solution)/shard_map/convert_element_type | solution.py:323
